TPU v7x, 32 devices: a whole 2x2x4 slice. The times are simulated.
32 devices in a mesh: seq: 8 (over z, y), tp: 4 (over x, core).
Axes of the slice: x: 2, y: 2, z: 4, core: 2. Of those that a mesh axis runs over, the one named last changes fastest.
Arguments:
- x_in: bfloat16 [1024, 8192], P('seq', 'tp'), may hold values from -6 to 6
- gate_in: bfloat16 [1024, 8192], P('seq', 'tp'), may hold values from -6 to 6
- conv_weight: float32 [4, 8192], P(None, 'tp'), may hold values from -3 to 3
- conv_bias: float32 [8192], P('tp'), may hold values from -0.5 to 0.5
- x_weight: bfloat16 [8192, 544], P('tp'), may hold values from -0.0625 to 0.0625
- dt_weight: bfloat16 [512, 8192], P(None, 'tp'), may hold values from -0.25 to 0.25
- dt_bias: float32 [8192], P('tp'), may hold values from -5 to -2.5
- decay_rate: float32 [8192, 16], P('tp'), may hold values from 0 to 4
- skip_gain: float32 [8192], P('tp'), may hold values from 0.5 to 1.5
- out_weight: bfloat16 [8192, 4096], P('tp'), may hold values from -0.0625 to 0.0625
- residual_in: bfloat16 [1024, 4096], P(('seq', 'tp')), may hold values from -36 to 36
- norm_gain: float32 [4096], replicated, may hold values from 0.1 to 1.9
- expert_ids: int32 [1024, 2], P(('seq', 'tp')), may hold values from 0 to 7, all different within a row; in each aligned block of 32 rows (0 to 31, 32 to 63, ...) at most 12 rows name the same one
- gate_prob: float32 [1024, 2], P(('seq', 'tp')), may hold values from 0.1 to 1
- up_weight: bfloat16 [4096, 98304], P(None, ('seq', 'tp')), may hold values from -0.09375 to 0.09375
- down_weight: bfloat16 [98304, 4096], P(('seq', 'tp')), may hold values from -0.0546875 to 0.0546875
Outputs:
- mixer_out: bfloat16 [1024, 4096], P(('seq', 'tp'))
- layer_out: bfloat16 [1024, 4096], P(('seq', 'tp'))
Inputs may be any that keep to these rules, and one draw needn't show every extreme that they name: `expert_ids`: each row names two different experts. In each device's aligned block of 32 rows no expert is named by more than 12 rows, a bound that some block reaches.
All inputs are finite; a program needn't handle non-finite values.
Results may differ from a plain program's by a relative error of at most 0.007.
Values may be sent and summed in bfloat16 or wider, within the bound.
A program may use at most 192 MiB of HBM per device.

v0:
```python
import jax
import jax.numpy as jnp
from jax import lax
from jax.sharding import PartitionSpec as P

STATE = 16
DTRANK = 512
EXPERTS = 8


def shifted(value, axis, steps):
    count = lax.axis_size(axis)
    initial, last = (max(0, -steps), min(count, count - steps))
    return lax.ppermute(value, axis, [(source, source + steps) for source in range(initial, last)])


def prefix(part, axis, combine, identity):
    place = lax.axis_index(axis)
    gathered = jax.tree.map(lambda a: lax.all_gather(a, axis), part)
    state = jax.tree.map(lambda a, e: jnp.zeros_like(a) + jnp.asarray(e, a.dtype), part, identity)

    def one(hop, state):
        return combine(
            state, jax.tree.map(lambda a: lax.dynamic_index_in_dim(a, hop, 0, False), gathered)
        )

    return lax.fori_loop(0, place, one, state)


def chain_join(earlier, later):
    return (earlier[0] * later[0], later[0] * earlier[1] + later[1])


def recur_blocks(start_state, step_cols, drive_cols, entry_cols, readout_cols, negative_rate):

    def advance(carried, columns):
        step_row, drive_row, entry_row, readout_row = columns
        carried = (
            jnp.exp(step_row[:, None, :] * negative_rate[None]) * carried
            + entry_row[:, :, None] * drive_row[:, None, :]
        )
        return (carried, jnp.sum(readout_row[:, :, None] * carried, axis=1))

    return lax.scan(advance, start_state, (step_cols, drive_cols, entry_cols, readout_cols))


def by_position(values, blocks, span):
    return values.reshape(blocks, span, values.shape[1]).transpose(1, 0, 2)


def expert_share(arrived_flat, up_weight, down_weight):
    hidden = jax.nn.silu(
        jnp.dot(arrived_flat, up_weight, preferred_element_type=jnp.float32)
    ).astype(jnp.bfloat16)
    return jnp.dot(hidden, down_weight, preferred_element_type=jnp.float32).astype(jnp.bfloat16)


def per_device(
    x_in,
    gate_in,
    conv_weight,
    conv_bias,
    x_weight,
    dt_weight,
    dt_bias,
    decay_rate,
    skip_gain,
    out_weight,
    residual_in,
    norm_gain,
    expert_ids,
    gate_prob,
    up_weight,
    down_weight,
):
    tokens, channels = x_in.shape
    width = out_weight.shape[1]
    reach = conv_weight.shape[0] - 1
    rim_rows = shifted(x_in[tokens - reach :], "seq", 1)
    padded = jnp.concatenate([rim_rows, x_in], axis=0).astype(jnp.float32)
    conv_out = conv_bias[None, :] + sum(
        (
            conv_weight[offset][None, :] * padded[offset : offset + tokens]
            for offset in range(reach + 1)
        )
    )
    inner = jax.nn.silu(conv_out).astype(jnp.bfloat16)
    projected = lax.psum(jnp.dot(inner, x_weight, preferred_element_type=jnp.float32), "tp")
    dt_low = projected[:, :DTRANK].astype(jnp.bfloat16)
    entry_rows = projected[:, DTRANK : DTRANK + STATE]
    readout_rows = projected[:, DTRANK + STATE :]
    step_size = jax.nn.softplus(
        jnp.dot(dt_low, dt_weight, preferred_element_type=jnp.float32) + dt_bias[None, :]
    )
    drive = step_size * inner.astype(jnp.float32)
    negative_rate = -decay_rate.T
    span = 16
    blocks = tokens // span
    step_cols = by_position(step_size, blocks, span)
    drive_cols = by_position(drive, blocks, span)
    entry_cols = by_position(entry_rows, blocks, span)
    readout_cols = by_position(readout_rows, blocks, span)
    zero_blocks = jnp.zeros((blocks, STATE, channels), jnp.float32)
    block_ends, local_out = recur_blocks(
        zero_blocks, step_cols, drive_cols, entry_cols, readout_cols, negative_rate
    )
    block_decay = jnp.exp(negative_rate[None] * jnp.sum(step_cols, axis=0)[:, None, :])
    decay_through, state_through = lax.associative_scan(
        chain_join, (block_decay, block_ends), axis=0
    )
    ones_state = jnp.ones((STATE, channels), jnp.float32)
    zeros_state = jnp.zeros((STATE, channels), jnp.float32)
    entering = prefix(
        (decay_through[-1], state_through[-1]), "seq", chain_join, (ones_state, zeros_state)
    )[1]
    decay_before = jnp.concatenate([ones_state[None], decay_through[:-1]], axis=0)
    state_before = jnp.concatenate([zeros_state[None], state_through[:-1]], axis=0)
    block_starts = decay_before * entering[None] + state_before
    ssm_cols = recur_blocks(
        block_starts, step_cols, drive_cols, entry_cols, readout_cols, negative_rate
    )[1]
    ssm = ssm_cols.transpose(1, 0, 2).reshape(tokens, channels)
    mixed = (
        (ssm + skip_gain[None, :] * inner.astype(jnp.float32))
        * jax.nn.silu(gate_in.astype(jnp.float32))
    ).astype(jnp.bfloat16)
    rows = tokens // lax.axis_size("tp")
    mixer_sum = lax.psum_scatter(
        jnp.dot(mixed, out_weight, preferred_element_type=jnp.float32),
        "tp",
        scatter_dimension=0,
        tiled=True,
    )
    mixer_out = (mixer_sum + residual_in.astype(jnp.float32)).astype(jnp.bfloat16)
    mixer_wide = mixer_out.astype(jnp.float32)
    normed = (
        mixer_wide
        * lax.rsqrt(jnp.mean(mixer_wide * mixer_wide, axis=1, keepdims=True) + 1e-06)
        * norm_gain[None, :]
    ).astype(jnp.bfloat16)
    seq_count = lax.axis_size("seq")
    devices = seq_count * lax.axis_size("tp")
    seq_group = seq_count // EXPERTS
    capacity = 3 * rows // EXPERTS
    chosen = expert_ids.reshape(-1)
    expert_hits = (chosen[:, None] == jnp.arange(EXPERTS, dtype=jnp.int32)[None, :]).astype(
        jnp.int32
    )
    earlier_hits = jnp.cumsum(expert_hits, axis=0) - expert_hits
    slot_index = jnp.sum(earlier_hits * expert_hits, axis=1)
    target = chosen * capacity + slot_index
    placing = (jnp.arange(EXPERTS * capacity, dtype=jnp.int32)[:, None] == target[None, :]).astype(
        jnp.bfloat16
    )
    placing = jnp.sum(placing.reshape(EXPERTS * capacity, rows, 2), axis=2)
    slots_out = (
        jnp.dot(placing, normed, preferred_element_type=jnp.float32)
        .astype(jnp.bfloat16)
        .reshape(EXPERTS, capacity, width)
    )
    along_seq = jnp.repeat(slots_out, seq_group, axis=0)
    arrived_seq = lax.all_to_all(along_seq, "seq", split_axis=0, concat_axis=0, tiled=True)
    arrived_all = lax.all_gather(
        arrived_seq.reshape(1, seq_count * capacity, width), "tp", axis=0, tiled=True
    )
    arrived_flat = arrived_all.reshape(devices * capacity, width)
    summed = lax.psum_scatter(
        expert_share(arrived_flat, up_weight, down_weight).astype(jnp.float32).astype(jnp.bfloat16),
        "tp",
        scatter_dimension=0,
        tiled=True,
    ).astype(jnp.float32)
    home = lax.all_to_all(
        summed.reshape(seq_count, capacity, width).astype(jnp.bfloat16),
        "seq",
        split_axis=0,
        concat_axis=0,
        tiled=True,
    ).astype(jnp.float32)
    expert_out = jnp.sum(home.reshape(EXPERTS, seq_group, capacity, width), axis=1).reshape(
        EXPERTS * capacity, width
    )
    picked = jnp.take(expert_out, target, axis=0).reshape(rows, 2, width)
    layer_out = (mixer_wide + jnp.sum(picked * gate_prob[:, :, None], axis=1)).astype(jnp.bfloat16)
    return (mixer_out, layer_out)


def solution(mesh):
    return jax.shard_map(
        per_device,
        mesh=mesh,
        in_specs=(
            P("seq", "tp"),
            P("seq", "tp"),
            P(None, "tp"),
            P("tp"),
            P("tp", None),
            P(None, "tp"),
            P("tp"),
            P("tp", None),
            P("tp"),
            P("tp", None),
            P(("seq", "tp"), None),
            P(),
            P(("seq", "tp"), None),
            P(("seq", "tp"), None),
            P(None, ("seq", "tp")),
            P(("seq", "tp"), None),
        ),
        out_specs=(P(("seq", "tp"), None), P(("seq", "tp"), None)),
        check_vma=False,
    )
```

profile of v0, /device:TPU:0, one launch (start us, length us, event | category | flops | bytes accessed | tf_op | source)
XLA Modules:
  0.0 464.8 jit_solution(15491746981362353329)
XLA Ops:
  7.2 0.9 slice.130
  8.1 4.9 %collective-permute-start = (bf16[3,2048]{1,0:T(4,128)(2,1)S(1)}, bf16[3,2048]{1,0:T(4,128)(2,1)S(1)}, u32[]{:S(2)}, u32[]{:S(2)}) collective-permute-start(bf16[3,2048]{1,0:T(4,128)(2,1)S(1)} %slice.130), channel_id=1, source_target_pairs={{0,4},{4,8},{8,12},{12,16},{16,20},{20,24},{24,28},{1,5},{5,9},{9,... | collective-permute-start | bytes 36872 | tf_op jit(solution)/shard_map/ppermute | solution.py:14
  13.0 0.9 fusion.36
  14.5 1.2 maximum_convert_fusion
  15.7 1.4 multiply_convert_fusion.2
  17.9 1.5 fusion.39
  19.5 33.8 %all-reduce.16.cloned.1.call-done = f32[128,544]{0,1:T(8,128)} async-done(((f32[128,544]{0,1:T(8,128)}), f32[128,544]{0,1:T(8,128)}) %all-reduce.16.cloned.1.call-update) | async-done | bytes 278544 | tf_op jit(solution)/shard_map/psum | solution.py:88
  53.3 2.7 convert_multiply_fusion.2
  56.6 2.6 copy_bitcast_fusion
  59.1 1.3 fusion.34
  60.6 22.9 %while.37 = (s32[]{:T(128)}, f32[8,16,2048]{2,1,0:T(8,128)S(1)}, f32[16,8,2048]{2,1,0:T(8,128)}, f32[16,2048]{1,0:T(8,128)S(1)}, f32[16,8,16]{2,1,0:T(8,128)S(1)...) while((s32[]{:T(128)}, f32[8,16,2048]{2,1,0:T(8,128)S(1)}, f32[16,8,2048]{2,1,0:T(8,128)}, ...), condition=%wide.region_3.4_spmd.clone, body=%wide.region_2.3_spmd.clone.sunk | while | flops 1310723 | bytes 2623079 | solution.py:44
  60.7 0.9 dynamic-slice_bitcast_fusion.13
  62.1 0.9 dynamic-slice_bitcast_fusion.13
  63.5 0.9 dynamic-slice_bitcast_fusion.13
  64.9 0.9 dynamic-slice_bitcast_fusion.13
  66.4 0.9 dynamic-slice_bitcast_fusion.13
  67.8 0.9 dynamic-slice_bitcast_fusion.13
  69.2 0.9 dynamic-slice_bitcast_fusion.13
  70.7 0.9 dynamic-slice_bitcast_fusion.13
  76.4 0.9 dynamic-slice_bitcast_fusion.13
  80.7 0.9 dynamic-slice_bitcast_fusion.13
  87.4 2.4 pad.48
  89.9 2.4 pad.49
  92.3 2.1 add.214
  94.4 4.2 pad.102
  98.5 1.6 pad_maximum_fusion.2
  100.1 2.4 pad.42
  102.6 2.4 pad.43
  105.0 2.2 add_multiply_fusion.1
  107.3 2.4 pad.50
  109.7 1.6 slice_add_fusion.3
  111.4 1.3 add.207
  112.7 2.3 pad.104
  115.0 1.6 slice.276
  116.7 2.3 pad.45
  119.0 2.4 pad.67
  121.4 1.9 pad_maximum_fusion
  123.3 4.2 pad.44
  128.4 2.4 slice_add_fusion.5
  130.8 1.0 slice_add_fusion
  131.9 20.2 %all-gather.6.cloned.1.call-done = f32[8,16,2048]{2,1,0:T(8,128)} async-done(((f32[1,16,2048]{2,1,0:T(8,128)}), f32[8,16,2048]{2,1,0:T(8,128)}) %all-gather.6.cloned.1.call-update) | async-done | bytes 1048592 | tf_op jit(solution)/shard_map/all_gather | solution.py:19
  152.1 41.6 %all-gather.4.cloned.1.call-done = f32[8,16,2048]{2,1,0:T(8,128)} async-done(((f32[1,16,2048]{2,1,0:T(8,128)}), f32[8,16,2048]{2,1,0:T(8,128)}) %all-gather.4.cloned.1.call-update) | async-done | bytes 1048592 | tf_op jit(solution)/shard_map/all_gather | solution.py:19
  193.9 1.3 pad_add_fusion
  195.3 36.9 %while.36 = (s32[]{:T(128)}, f32[8,16,2048]{2,1,0:T(8,128)S(1)}, f32[16,8,2048]{2,1,0:T(8,128)}, f32[16,8,2048]{2,1,0:T(8,128)}, f32[16,2048]{1,0:T(8,128)S(1)},...) while((s32[]{:T(128)}, f32[8,16,2048]{2,1,0:T(8,128)S(1)}, ...), condition=%wide.region_8.9_spmd, body=%wide.region_6.8_spmd.sunk | while | flops 1556482 | bytes 2821733 | solution.py:44
  195.3 0.9 dynamic-slice_bitcast_fusion.12
  232.2 1.8 copy.55
  234.1 1.0 fusion.4
  235.1 9.5 %fusion.40 = f32[128,4096]{1,0:T(8,128)} fusion(bf16[128,2048]{1,0:T(8,128)(2,1)S(1)} %fusion.4, bf16[2048,4096]{1,0:T(8,128)(2,1)} %param.31), kind=kOutput, calls=%fused_computation.108 | convolution fusion | flops 2147483648 | bytes 19398656 | tf_op jit(solution)/shard_map/dot_general | solution.py:129
  245.6 36.9 %reduce-scatter.3.cloned.1.call-done = f32[32,4096]{1,0:T(8,128)} async-done(((f32[128,4096]{1,0:T(8,128)}), f32[32,4096]{1,0:T(8,128)}) %reduce-scatter.3.cloned.1.call-update) | async-done | bytes 524304 | tf_op jit(solution)/shard_map/reduce_scatter | solution.py:128
  282.4 1.2 fusion.12
  285.0 31.1 %all_to_all.10 = bf16[8,12,4096]{2,1,0:T(8,128)(2,1)S(1)} all-to-all(bf16[8,12,4096]{2,1,0:T(8,128)(2,1)S(1)} %reshape_broadcast_in_dim_reshape.3), channel_id=1, replica_groups=mesh['seq'=8,'tp'=4] {'seq'}, dimensions={0} | all-to-all | bytes 1572864 | tf_op jit(solution)/shard_map/all_to_all | solution.py:162
  316.1 1.1 reshape.138
  317.4 26.5 %all-gather.8.cloned.1.call-done = bf16[4,96,4096]{2,1,0:T(8,128)(2,1)} async-done(((bf16[1,96,4096]{2,1,0:T(8,128)(2,1)}), bf16[4,96,4096]{2,1,0:T(8,128)(2,1)}) %all-gather.8.cloned.1.call-update) | async-done | bytes 3145744 | tf_op jit(solution)/shard_map/all_gather | solution.py:163
  343.9 16.0 %multiply_convert_fusion.5 = bf16[384,3072]{1,0:T(8,128)(2,1)S(1)} fusion(bf16[384,4096]{1,0:T(8,128)(2,1)} %bitcast.97, bf16[4096,3072]{1,0:T(8,128)(2,1)} %param.36), kind=kOutput, calls=%fused_computation.16.clone.clone.1 | convolution fusion | flops 9669574656 | bytes 30670848 | tf_op jit(solution)/shard_map/dot_general | solution.py:53
  360.0 15.9 %convolution_convert_fusion = bf16[384,4096]{1,0:T(8,128)(2,1)} fusion(bf16[3072,4096]{1,0:T(8,128)(2,1)} %param.37, bf16[384,3072]{1,0:T(8,128)(2,1)S(1)} %multiply_convert_fusion.5), kind=kOutput, calls=%fused_computation.15 | convolution fusion | flops 9665249280 | bytes 30670848 | tf_op jit(solution)/shard_map/dot_general | solution.py:55
  375.9 38.1 %reduce-scatter.5.cloned.1.call-done = bf16[96,4096]{1,0:T(8,128)(2,1)} async-done(((bf16[384,4096]{1,0:T(8,128)(2,1)}), bf16[96,4096]{1,0:T(8,128)(2,1)}) %reduce-scatter.5.cloned.1.call-update) | async-done | bytes 786448 | tf_op jit(solution)/shard_map/reduce_scatter | solution.py:167
  414.0 2.2 convert_element_type.72
  416.2 5.5 %all-to-all-start.1 = ((bf16[8,12,4096]{2,1,0:T(8,128)(2,1)}), bf16[8,12,4096]{2,1,0:T(8,128)(2,1)S(1)}, u32[]{:S(2)}, u32[]{:S(2)}) async-start(bf16[8,12,4096]{2,1,0:T(8,128)(2,1)} %convert_element_type.72), calls=%async_computation.3 | async-start | bytes 2097152 | tf_op jit(solution)/shard_map/all_to_all | solution.py:173
  422.1 25.4 %all-to-all-done.1 = bf16[8,12,4096]{2,1,0:T(8,128)(2,1)S(1)} async-done(((bf16[8,12,4096]{2,1,0:T(8,128)(2,1)}), bf16[8,12,4096]{2,1,0:T(8,128)(2,1)S(1)}, u32[]{:S(2)}, u32[]{:S(2)}) %all-to-all-start.1) | async-done | bytes 786464 | tf_op jit(solution)/shard_map/all_to_all | solution.py:173
  447.5 1.4 reshape.143
  448.8 2.9 gather_fusion
  451.8 1.6 gather.7
  453.4 2.9 multiply_reduce_fusion.1
  456.3 1.7 fusion.15
  (198 shorter events, 59.3 us)
Async XLA Ops:
  7.2 10.8 %copy-start = (bf16[2048,544]{0,1:T(8,128)(2,1)S(1)}, bf16[2048,544]{0,1:T(8,128)(2,1)}, u32[]{:S(2)}) copy-start(bf16[2048,544]{0,1:T(8,128)(2,1)} %param.26) | copy-start | bytes 6684676
  7.2 46.1 %all-reduce.16.cloned.1.call-start = ((), (), s32[]{:S(2)}) async-start(), calls=%async_computation.4 | async-start | bytes 557056 | tf_op jit(solution)/shard_map/psum | solution.py:88
  8.1 6.3 %collective-permute-start = (bf16[3,2048]{1,0:T(4,128)(2,1)S(1)}, bf16[3,2048]{1,0:T(4,128)(2,1)S(1)}, u32[]{:S(2)}, u32[]{:S(2)}) collective-permute-start(bf16[3,2048]{1,0:T(4,128)(2,1)S(1)} %slice.130), channel_id=1, source_target_pairs={{0,4},{4,8},{8,12},{12,16},{16,20},{20,24},{24,28},{1,5},{5,9},{9,... | collective-permute-start | bytes 36872 | tf_op jit(solution)/shard_map/ppermute | solution.py:14
  14.0 3.1 copy-start.12
  14.0 3.1 copy-start.14
  15.6 3.8 copy-start.11
  15.7 37.6 %copy-start.19 = (f32[2048]{0:T(1024)S(1)}, f32[2048]{0:T(1024)}, u32[]{:S(2)}) copy-start(f32[2048]{0:T(1024)} %param.28) | copy-start | bytes 24580
  17.1 0.8 copy-start.2
  19.4 132.7 %all-gather.6.cloned.1.call-start = ((), (), s32[]{:S(2)}) async-start(), calls=%async_computation.6 | async-start | bytes 1179648 | tf_op jit(solution)/shard_map/all_gather | solution.py:19
  100.1 7.1 %copy-start.9 = (f32[1,16,2048]{2,1,0:T(8,128)S(1)}, f32[1,16,2048]{2,1,0:T(8,128)}, u32[]{:S(2)}) copy-start(f32[1,16,2048]{2,1,0:T(8,128)} %slice.154) | copy-start | bytes 393220
  111.4 82.4 %all-gather.4.cloned.1.call-start = ((), (), s32[]{:S(2)}) async-start(), calls=%async_computation.5 | async-start | bytes 1179648 | tf_op jit(solution)/shard_map/all_gather | solution.py:19
  116.6 165.9 %reduce-scatter.3.cloned.1.call-start = ((), (), s32[]{:S(2)}) async-start(), calls=%async_computation.7 | async-start | bytes 2621440 | tf_op jit(solution)/shard_map/reduce_scatter | solution.py:128
  116.7 11.8 %copy-start.3 = (f32[8,16,2048]{2,1,0:T(8,128)S(1)}, f32[8,16,2048]{2,1,0:T(8,128)}, u32[]{:S(2)}) copy-start(f32[8,16,2048]{2,1,0:T(8,128)} %pad.102) | copy-start | bytes 3145732
  121.4 9.4 %copy-start.4 = (f32[8,16,2048]{2,1,0:T(8,128)S(1)}, f32[8,16,2048]{2,1,0:T(8,128)}, u32[]{:S(2)}) copy-start(f32[8,16,2048]{2,1,0:T(8,128)} %pad.45) | copy-start | bytes 3145732
  128.4 2.4 copy-start.5
  130.8 63.1 %copy-start.6 = (f32[7,16,2048]{2,1,0:T(8,128)S(1)}, f32[7,16,2048]{2,1,0:T(8,128)}, u32[]{:S(2)}) copy-start(f32[7,16,2048]{2,1,0:T(8,128)} %slice_add_fusion.5) | copy-start | bytes 2752516
  195.3 38.8 %copy-start.8 = (bf16[128,2048]{1,0:T(8,128)(2,1)S(1)}, bf16[128,2048]{1,0:T(8,128)(2,1)}, u32[]{:S(2)}) copy-start(bf16[128,2048]{1,0:T(8,128)(2,1)} %param.23) | copy-start | bytes 1572868
  195.3 38.8 %copy-start.13 = (f32[1,2048]{1,0:T(1,128)S(1)}, f32[1,2048]{1,0:T(1,128)}, u32[]{:S(2)}) copy-start(f32[1,2048]{1,0:T(1,128)} %copy-done.12) | copy-start | bytes 24580
  195.3 38.8 %copy-start.15 = (f32[1,2048]{1,0:T(1,128)S(1)}, f32[1,2048]{1,0:T(1,128)}, u32[]{:S(2)}) copy-start(f32[1,2048]{1,0:T(1,128)} %copy-done.14) | copy-start | bytes 24580
  195.3 38.8 %copy-start.16 = (f32[2048]{0:T(1024)S(1)}, f32[2048]{0:T(1024)}, u32[]{:S(2)}) copy-start(f32[2048]{0:T(1024)} %param.25) | copy-start | bytes 24580
  195.3 38.8 %copy-start.20 = (f32[2048]{0:T(1024)S(1)}, f32[2048]{0:T(1024)}, u32[]{:S(2)}) copy-start(f32[2048]{0:T(1024)} %param.30) | copy-start | bytes 24580
  235.1 9.6 %copy-start.18 = (s32[32,2]{0,1:T(2,128)S(1)}, s32[32,2]{0,1:T(2,128)}, u32[]{:S(2)}) copy-start(s32[32,2]{0,1:T(2,128)} %param.34) | copy-start | bytes 772
  235.1 47.3 %copy-start.10 = (bf16[32,4096]{1,0:T(8,128)(2,1)S(1)}, bf16[32,4096]{1,0:T(8,128)(2,1)}, u32[]{:S(2)}) copy-start(bf16[32,4096]{1,0:T(8,128)(2,1)} %param.32) | copy-start | bytes 786436
  244.6 39.7 %copy-start.17 = (f32[4096]{0:T(1024)S(1)}, f32[4096]{0:T(1024)}, u32[]{:S(2)}) copy-start(f32[4096]{0:T(1024)} %param.33) | copy-start | bytes 49156
  244.7 99.3 %all-gather.8.cloned.1.call-start = ((), (), s32[]{:S(2)}) async-start(), calls=%async_computation.8 | async-start | bytes 3932160 | tf_op jit(solution)/shard_map/all_gather | solution.py:163
  283.7 0.7 copy-start.7
  317.2 96.8 %reduce-scatter.5.cloned.1.call-start = ((), (), s32[]{:S(2)}) async-start(), calls=%async_computation.9 | async-start | bytes 3932160 | tf_op jit(solution)/shard_map/reduce_scatter | solution.py:167
  375.9 46.1 %copy-start.21 = (f32[32,2]{0,1:T(2,128)S(1)}, f32[32,2]{0,1:T(2,128)}, u32[]{:S(2)}) copy-start(f32[32,2]{0,1:T(2,128)} %param.35) | copy-start | bytes 772
  416.2 31.3 %all-to-all-start.1 = ((bf16[8,12,4096]{2,1,0:T(8,128)(2,1)}), bf16[8,12,4096]{2,1,0:T(8,128)(2,1)S(1)}, u32[]{:S(2)}, u32[]{:S(2)}) async-start(bf16[8,12,4096]{2,1,0:T(8,128)(2,1)} %convert_element_type.72), calls=%async_computation.3 | async-start | bytes 2097152 | tf_op jit(solution)/shard_map/all_to_all | solution.py:173
  448.8 9.1 %copy-start.1 = (bf16[2048,544]{0,1:T(8,128)(2,1)S(1)}, bf16[2048,544]{0,1:T(8,128)(2,1)}, u32[]{:S(2)}) copy-start(bf16[2048,544]{0,1:T(8,128)(2,1)} %param.26) | copy-start | bytes 6684676
Sparse Core Ops, SparseCore 0:
  19.5 33.7 all-reduce.15
  111.5 40.5 all-gather.5
  154.8 38.8 all-gather.3
  244.8 37.5 reduce-scatter.2
  317.3 26.5 all-gather.7
  376.0 37.9 reduce-scatter.4
where the time goes:
time: 467 us; the launch traced here: 465 us
  waiting for transfers between devices  223 us (48%)
  local copies, waits for them, and re-layouts  88.8 us (19%)
  other arithmetic  49.3 us (11%)
  matrix products  46.1 us (10%)
  blocking collectives  31.1 us (7%)
  between operations  14.6 us (3%)
  starting transfers between devices  10.9 us (2%)
    all_gather x2, waiting for transfers between devices, prefix(): gathered = jax.tree.map(lambda a: lax.all_gather(a, axis), part)  61.9 us
    reduce_scatter x1, waiting for transfers between devices, per_device(): lax.psum_scatter(expert_share(arrived_flat, up_weight, down_weight).astyp...  38.1 us
    reduce_scatter x1, waiting for transfers between devices, per_device(): lax.psum_scatter(jnp.dot(mixed, out_weight, preferred_element_type=jnp.fl...  36.9 us
    psum x1, waiting for transfers between devices, per_device(): lax.psum(jnp.dot(inner, x_weight, preferred_element_type=jnp.float32), 'tp')  33.8 us
    all_to_all x1, blocking collectives, per_device(): lax.all_to_all(along_seq, 'seq', split_axis=0, concat_axis=0, tiled=True)  31.1 us
    mul x48, local copies, waits for them, and re-layouts, advance(): entry_row[:, :, None] * drive_row[:, None, :]  28.5 us
    all_gather x1, waiting for transfers between devices, per_device(): lax.all_gather(arrived_seq.reshape(1, seq_count * capacity, width), 'tp',...  26.5 us
    all_to_all x1, waiting for transfers between devices, per_device(): lax.all_to_all(summed.reshape(seq_count, capacity, width).astype(jnp.bflo...  25.4 us
  transfers between devices with their start and end apart: 8, of which 8 were waited for; matrix products, arithmetic and copies ran while one was open for 5% of the time, Pallas kernels for 0%

commit v1 on v0

--- a/solution.py
+++ b/solution.py
@@ -6,6 +6,28 @@
 STATE = 16
 DTRANK = 512
 EXPERTS = 8
+
+
+def laid_out(tiles, dim):
+    dims = list(tiles.shape[1:])
+    dims[dim] *= tiles.shape[0]
+    return jnp.moveaxis(tiles, 0, dim).reshape(dims)
+
+
+def doubled(x, axis):
+    size = lax.axis_size(axis)
+    pieces = x[None]
+    for level in range(size.bit_length() - 1):
+        bit = 1 << level
+        other = lax.ppermute(pieces, axis, [(i, i ^ bit) for i in range(size)])
+        both = jnp.stack([pieces, other])
+        upper = lax.axis_index(axis) >> level & 1
+        pieces = jnp.where(upper == 0, both, both[::-1]).reshape(-1, *x.shape)
+    return pieces
+
+
+def collect(shard, axis, dim):
+    return laid_out(doubled(shard, axis), dim)
 
 
 def shifted(value, axis, steps):
@@ -160,9 +182,7 @@
     )
     along_seq = jnp.repeat(slots_out, seq_group, axis=0)
     arrived_seq = lax.all_to_all(along_seq, "seq", split_axis=0, concat_axis=0, tiled=True)
-    arrived_all = lax.all_gather(
-        arrived_seq.reshape(1, seq_count * capacity, width), "tp", axis=0, tiled=True
-    )
+    arrived_all = collect(arrived_seq.reshape(1, seq_count * capacity, width), "tp", 0)
     arrived_flat = arrived_all.reshape(devices * capacity, width)
     summed = lax.psum_scatter(
         expert_share(arrived_flat, up_weight, down_weight).astype(jnp.float32).astype(jnp.bfloat16),

time: 467 us -> 483 us (1.034)
  waiting for transfers between devices: 223 us -> 233 us
  other arithmetic: 49.3 us -> 54.2 us
    ppermute x0 -> x2, waiting for transfers between devices: none -> 38.1 us  [doubled(): other = lax.ppermute(pieces, axis, [(i, i ^ bit) for i in range(size)])]
    all_gather x1 -> x0, waiting for transfers between devices: 26.5 us -> none  [per_device(): lax.all_gather(arrived_seq.reshape(1, seq_count * capacity, width), 'tp',...]
    another operation x0 -> x3, other arithmetic: none -> 5.08 us  [doubled(): both = jnp.stack([pieces, other])]
  transfers between devices with their start and end apart: 8 -> 9, of which waited for: 8 -> 9; matrix products, arithmetic and copies ran while one was open for 5% -> 5% of each run, Pallas kernels for 0% -> 0%
where the time goes in v1:
time: 483 us; the launch traced here: 480 us
  waiting for transfers between devices  233 us (48%)
  local copies, waits for them, and re-layouts  90.1 us (19%)
  other arithmetic  54.2 us (11%)
  matrix products  45.2 us (9%)
  blocking collectives  31.1 us (6%)
  between operations  14.3 us (3%)
  starting transfers between devices  11.2 us (2%)
    all_gather x2, waiting for transfers between devices, prefix(): gathered = jax.tree.map(lambda a: lax.all_gather(a, axis), part)  61.8 us
    ppermute x2, waiting for transfers between devices, doubled(): other = lax.ppermute(pieces, axis, [(i, i ^ bit) for i in range(size)])  38.1 us
    reduce_scatter x1, waiting for transfers between devices, per_device(): lax.psum_scatter(jnp.dot(mixed, out_weight, preferred_element_type=jnp.fl...  36.9 us
    reduce_scatter x1, waiting for transfers between devices, per_device(): lax.psum_scatter(expert_share(arrived_flat, up_weight, down_weight).astyp...  36.2 us
    psum x1, waiting for transfers between devices, per_device(): lax.psum(jnp.dot(inner, x_weight, preferred_element_type=jnp.float32), 'tp')  33.8 us
    all_to_all x1, blocking collectives, per_device(): lax.all_to_all(along_seq, 'seq', split_axis=0, concat_axis=0, tiled=True)  31.1 us
    mul x48, local copies, waits for them, and re-layouts, advance(): entry_row[:, :, None] * drive_row[:, None, :]  28.4 us
    all_to_all x1, waiting for transfers between devices, per_device(): lax.all_to_all(summed.reshape(seq_count, capacity, width).astype(jnp.bflo...  25.3 us
  transfers between devices with their start and end apart: 9, of which 9 were waited for; matrix products, arithmetic and copies ran while one was open for 5% of the time, Pallas kernels for 0%

profile of v1, /device:TPU:0, one launch (start us, length us, event | category | flops | bytes accessed | tf_op | source)
XLA Modules:
  0.0 479.7 jit_solution(2106598207567066338)
XLA Ops:
  7.2 0.9 slice.130
  8.1 4.9 %collective-permute-start = (bf16[3,2048]{1,0:T(4,128)(2,1)S(1)}, bf16[3,2048]{1,0:T(4,128)(2,1)S(1)}, u32[]{:S(2)}, u32[]{:S(2)}) collective-permute-start(bf16[3,2048]{1,0:T(4,128)(2,1)S(1)} %slice.130), channel_id=1, source_target_pairs={{0,4},{4,8},{8,12},{12,16},{16,20},{20,24},{24,28},{1,5},{5,9},{9,... | collective-permute-start | bytes 36872 | tf_op jit(solution)/shard_map/ppermute | solution.py:36
  13.0 0.9 fusion.38
  14.5 1.2 maximum_convert_fusion
  15.6 1.4 multiply_convert_fusion.2
  17.8 1.5 fusion.41
  19.4 33.8 %all-reduce.16.cloned.1.call-done = f32[128,544]{0,1:T(8,128)} async-done(((f32[128,544]{0,1:T(8,128)}), f32[128,544]{0,1:T(8,128)}) %all-reduce.16.cloned.1.call-update) | async-done | bytes 278544 | tf_op jit(solution)/shard_map/psum | solution.py:110
  53.2 2.7 convert_multiply_fusion.2
  56.5 2.6 copy_bitcast_fusion
  59.1 1.3 fusion.36
  60.6 22.9 %while.37 = (s32[]{:T(128)}, f32[8,16,2048]{2,1,0:T(8,128)S(1)}, f32[16,8,2048]{2,1,0:T(8,128)}, f32[16,2048]{1,0:T(8,128)S(1)}, f32[16,8,16]{2,1,0:T(8,128)S(1)...) while((s32[]{:T(128)}, f32[8,16,2048]{2,1,0:T(8,128)S(1)}, f32[16,8,2048]{2,1,0:T(8,128)}, ...), condition=%wide.region_3.4_spmd.clone, body=%wide.region_2.3_spmd.clone.sunk | while | flops 1310723 | bytes 2623079 | solution.py:66
  60.6 0.9 dynamic-slice_bitcast_fusion.13
  62.0 0.9 dynamic-slice_bitcast_fusion.13
  63.4 0.9 dynamic-slice_bitcast_fusion.13
  64.9 0.9 dynamic-slice_bitcast_fusion.13
  66.3 0.9 dynamic-slice_bitcast_fusion.13
  76.3 0.9 dynamic-slice_bitcast_fusion.13
  80.6 0.9 dynamic-slice_bitcast_fusion.13
  87.5 2.4 pad.48
  89.9 2.4 pad.49
  92.4 2.1 add.214
  94.4 4.2 pad.110
  98.6 1.6 pad_maximum_fusion.4
  100.2 2.4 pad.42
  102.6 2.4 pad.43
  105.1 2.3 add_multiply_fusion.1
  107.4 2.4 pad.50
  109.8 1.6 slice_add_fusion.3
  111.5 1.3 add.207
  112.8 2.3 pad.112
  115.1 1.6 slice.276
  116.8 2.5 pad.45
  119.3 4.1 pad.71
  124.3 4.1 pad.44
  128.6 2.3 slice_add_fusion.5
  131.0 1.0 slice_add_fusion
  132.0 20.2 %all-gather.5.cloned.1.call-done = f32[8,16,2048]{2,1,0:T(8,128)} async-done(((f32[1,16,2048]{2,1,0:T(8,128)}), f32[8,16,2048]{2,1,0:T(8,128)}) %all-gather.5.cloned.1.call-update) | async-done | bytes 1048592 | tf_op jit(solution)/shard_map/all_gather | solution.py:41
  152.2 41.6 %all-gather.3.cloned.1.call-done = f32[8,16,2048]{2,1,0:T(8,128)} async-done(((f32[1,16,2048]{2,1,0:T(8,128)}), f32[8,16,2048]{2,1,0:T(8,128)}) %all-gather.3.cloned.1.call-update) | async-done | bytes 1048592 | tf_op jit(solution)/shard_map/all_gather | solution.py:41
  194.1 1.3 pad_add_fusion
  195.4 37.0 %while.36 = (s32[]{:T(128)}, f32[8,16,2048]{2,1,0:T(8,128)S(1)}, f32[16,8,2048]{2,1,0:T(8,128)}, f32[16,8,2048]{2,1,0:T(8,128)}, f32[16,2048]{1,0:T(8,128)S(1)},...) while((s32[]{:T(128)}, f32[8,16,2048]{2,1,0:T(8,128)S(1)}, ...), condition=%wide.region_8.9_spmd, body=%wide.region_6.8_spmd.sunk | while | flops 1556482 | bytes 2821733 | solution.py:66
  195.4 0.9 dynamic-slice_bitcast_fusion.12
  232.5 1.9 copy.55
  234.4 1.0 fusion.6
  235.4 9.5 %fusion.42 = f32[128,4096]{1,0:T(8,128)} fusion(bf16[128,2048]{1,0:T(8,128)(2,1)S(1)} %fusion.6, bf16[2048,4096]{1,0:T(8,128)(2,1)} %param.31), kind=kOutput, calls=%fused_computation.114 | convolution fusion | flops 2147483648 | bytes 19398656 | tf_op jit(solution)/shard_map/dot_general | solution.py:151
  245.8 36.9 %reduce-scatter.3.cloned.1.call-done = f32[32,4096]{1,0:T(8,128)} async-done(((f32[128,4096]{1,0:T(8,128)}), f32[32,4096]{1,0:T(8,128)}) %reduce-scatter.3.cloned.1.call-update) | async-done | bytes 524304 | tf_op jit(solution)/shard_map/reduce_scatter | solution.py:150
  282.7 1.2 fusion.14
  284.8 31.1 %all_to_all.10 = bf16[8,12,4096]{2,1,0:T(8,128)(2,1)S(1)} all-to-all(bf16[8,12,4096]{2,1,0:T(8,128)(2,1)S(1)} %reshape_broadcast_in_dim_reshape.3), channel_id=1, replica_groups=mesh['seq'=8,'tp'=4] {'seq'}, dimensions={0} | all-to-all | bytes 1572864 | tf_op jit(solution)/shard_map/all_to_all | solution.py:184
  316.3 2.2 collective-permute-done.1
  318.6 1.3 pad_maximum_fusion.1
  319.8 1.6 fusion.3
  322.0 35.9 %collective-permute-done.2 = bf16[2,1,96,4096]{3,2,0,1:T(8,128)(2,1)S(1)} collective-permute-done((bf16[2,1,96,4096]{3,2,0,1:T(8,128)(2,1)S(1)}, bf16[2,1,96,4096]{3,2,0,1:T(8,128)(2,1)S(1)}, u32[]{:S(2)}, u32[]{:S(2)}) %collective-permute-start.2) | collective-permute-done | bytes 1572896 | tf_op jit(solution)/shard_map/ppermute | solution.py:22
  357.9 1.1 copy-done.11
  359.1 2.2 pad_maximum_fusion
  362.0 15.2 %multiply_convert_fusion.5 = bf16[384,3072]{1,0:T(8,128)(2,1)S(1)} fusion(bf16[384,4096]{1,0:T(8,128)(2,1)S(1)} %bitcast.92, bf16[4096,3072]{1,0:T(8,128)(2,1)} %param.36), kind=kOutput, calls=%fused_computation.17.clone.clone.1 | convolution fusion | flops 9669574656 | bytes 30670848 | tf_op jit(solution)/shard_map/dot_general | solution.py:75
  377.2 15.8 %convolution_convert_fusion = bf16[384,4096]{1,0:T(8,128)(2,1)} fusion(bf16[3072,4096]{1,0:T(8,128)(2,1)} %param.37, bf16[384,3072]{1,0:T(8,128)(2,1)S(1)} %multiply_convert_fusion.5), kind=kOutput, calls=%fused_computation.15 | convolution fusion | flops 9665249280 | bytes 30670848 | tf_op jit(solution)/shard_map/dot_general | solution.py:77
  393.1 36.2 %reduce-scatter.5.cloned.1.call-done = bf16[96,4096]{1,0:T(8,128)(2,1)} async-done(((bf16[384,4096]{1,0:T(8,128)(2,1)}), bf16[96,4096]{1,0:T(8,128)(2,1)}) %reduce-scatter.5.cloned.1.call-update) | async-done | bytes 786448 | tf_op jit(solution)/shard_map/reduce_scatter | solution.py:187
  429.3 2.2 convert_element_type.72
  431.5 5.5 %all-to-all-start.1 = ((bf16[8,12,4096]{2,1,0:T(8,128)(2,1)}), bf16[8,12,4096]{2,1,0:T(8,128)(2,1)S(1)}, u32[]{:S(2)}, u32[]{:S(2)}) async-start(bf16[8,12,4096]{2,1,0:T(8,128)(2,1)} %convert_element_type.72), calls=%async_computation.3 | async-start | bytes 2097152 | tf_op jit(solution)/shard_map/all_to_all | solution.py:193
  437.4 25.3 %all-to-all-done.1 = bf16[8,12,4096]{2,1,0:T(8,128)(2,1)S(1)} async-done(((bf16[8,12,4096]{2,1,0:T(8,128)(2,1)}), bf16[8,12,4096]{2,1,0:T(8,128)(2,1)S(1)}, u32[]{:S(2)}, u32[]{:S(2)}) %all-to-all-start.1) | async-done | bytes 786464 | tf_op jit(solution)/shard_map/all_to_all | solution.py:193
  462.7 1.4 reshape.139
  464.1 2.9 gather_fusion
  467.0 1.6 gather.7
  468.6 2.9 multiply_reduce_fusion.1
  471.5 1.7 fusion.17
  (215 shorter events, 63.4 us)
Async XLA Ops:
  7.2 10.7 %copy-start = (bf16[2048,544]{0,1:T(8,128)(2,1)S(1)}, bf16[2048,544]{0,1:T(8,128)(2,1)}, u32[]{:S(2)}) copy-start(bf16[2048,544]{0,1:T(8,128)(2,1)} %param.26) | copy-start | bytes 6684676
  7.2 46.0 %all-reduce.16.cloned.1.call-start = ((), (), s32[]{:S(2)}) async-start(), calls=%async_computation.4 | async-start | bytes 557056 | tf_op jit(solution)/shard_map/psum | solution.py:110
  8.1 6.3 %collective-permute-start = (bf16[3,2048]{1,0:T(4,128)(2,1)S(1)}, bf16[3,2048]{1,0:T(4,128)(2,1)S(1)}, u32[]{:S(2)}, u32[]{:S(2)}) collective-permute-start(bf16[3,2048]{1,0:T(4,128)(2,1)S(1)} %slice.130), channel_id=1, source_target_pairs={{0,4},{4,8},{8,12},{12,16},{16,20},{20,24},{24,28},{1,5},{5,9},{9,... | collective-permute-start | bytes 36872 | tf_op jit(solution)/shard_map/ppermute | solution.py:36
  14.0 3.0 copy-start.16
  14.0 3.0 copy-start.18
  17.0 0.8 copy-start.3
  17.8 1.5 copy-start.15
  17.8 35.4 %copy-start.24 = (f32[2048]{0:T(1024)S(1)}, f32[2048]{0:T(1024)}, u32[]{:S(2)}) copy-start(f32[2048]{0:T(1024)} %param.28) | copy-start | bytes 24580
  19.3 132.9 %all-gather.5.cloned.1.call-start = ((), (), s32[]{:S(2)}) async-start(), calls=%async_computation.6 | async-start | bytes 1179648 | tf_op jit(solution)/shard_map/all_gather | solution.py:41
  83.6 33.2 %copy-start.2 = (f32[8,16,2048]{2,1,0:T(8,128)}, f32[8,16,2048]{2,1,0:T(8,128)S(1)}, u32[]{:S(2)}) copy-start(f32[8,16,2048]{2,1,0:T(8,128)S(1)} %multiply_exponential_fusion) | copy-start | bytes 3145732
  100.2 7.1 %copy-start.13 = (f32[1,16,2048]{2,1,0:T(8,128)S(1)}, f32[1,16,2048]{2,1,0:T(8,128)}, u32[]{:S(2)}) copy-start(f32[1,16,2048]{2,1,0:T(8,128)} %slice.154) | copy-start | bytes 393220
  107.4 4.1 copy-start.4
  111.5 82.4 %all-gather.3.cloned.1.call-start = ((), (), s32[]{:S(2)}) async-start(), calls=%async_computation.5 | async-start | bytes 1179648 | tf_op jit(solution)/shard_map/all_gather | solution.py:41
  112.8 10.7 %copy-start.10 = (f32[3,16,2048]{2,1,0:T(8,128)S(1)}, f32[3,16,2048]{2,1,0:T(8,128)}, u32[]{:S(2)}) copy-start(f32[3,16,2048]{2,1,0:T(8,128)} %get-tuple-element.196) | copy-start | bytes 1179652
  116.7 165.9 %reduce-scatter.3.cloned.1.call-start = ((), (), s32[]{:S(2)}) async-start(), calls=%async_computation.7 | async-start | bytes 2621440 | tf_op jit(solution)/shard_map/reduce_scatter | solution.py:150
  116.8 6.6 %slice-start = ((f32[8,16,2048]{2,1,0:T(8,128)}), f32[1,16,2048]{2,1,0:T(8,128)S(1)}, s32[]{:S(2)}) async-start(f32[8,16,2048]{2,1,0:T(8,128)} %copy-done.2), calls=%async_computation.9 | async-start | bytes 262144 | tf_op jit(solution)/shard_map/slice | solution.py:130
  119.3 9.1 %copy-start.21 = (f32[128,16]{0,1:T(8,128)S(1)}, f32[128,16]{0,1:T(8,128)}, u32[]{:S(2)}) copy-start(f32[128,16]{0,1:T(8,128)} %get-tuple-element.206) | copy-start | bytes 24580
  119.3 9.3 %copy-start.5 = (f32[8,16,2048]{2,1,0:T(8,128)S(1)}, f32[8,16,2048]{2,1,0:T(8,128)}, u32[]{:S(2)}) copy-start(f32[8,16,2048]{2,1,0:T(8,128)} %pad.110) | copy-start | bytes 3145732
  124.3 6.7 %copy-start.6 = (f32[8,16,2048]{2,1,0:T(8,128)S(1)}, f32[8,16,2048]{2,1,0:T(8,128)}, u32[]{:S(2)}) copy-start(f32[8,16,2048]{2,1,0:T(8,128)} %pad.45) | copy-start | bytes 3145732
  128.6 2.4 copy-start.7
  131.0 63.1 %copy-start.8 = (f32[7,16,2048]{2,1,0:T(8,128)S(1)}, f32[7,16,2048]{2,1,0:T(8,128)}, u32[]{:S(2)}) copy-start(f32[7,16,2048]{2,1,0:T(8,128)} %slice_add_fusion.5) | copy-start | bytes 2752516
  195.4 39.0 %copy-start.17 = (f32[1,2048]{1,0:T(1,128)S(1)}, f32[1,2048]{1,0:T(1,128)}, u32[]{:S(2)}) copy-start(f32[1,2048]{1,0:T(1,128)} %copy-done.16) | copy-start | bytes 24580
  195.4 39.0 %copy-start.19 = (f32[1,2048]{1,0:T(1,128)S(1)}, f32[1,2048]{1,0:T(1,128)}, u32[]{:S(2)}) copy-start(f32[1,2048]{1,0:T(1,128)} %copy-done.18) | copy-start | bytes 24580
  195.4 39.0 %copy-start.20 = (f32[2048]{0:T(1024)S(1)}, f32[2048]{0:T(1024)}, u32[]{:S(2)}) copy-start(f32[2048]{0:T(1024)} %param.25) | copy-start | bytes 24580
  195.4 39.0 %copy-start.25 = (f32[2048]{0:T(1024)S(1)}, f32[2048]{0:T(1024)}, u32[]{:S(2)}) copy-start(f32[2048]{0:T(1024)} %param.30) | copy-start | bytes 24580
  232.5 1.9 copy-start.12
  235.4 9.6 %copy-start.23 = (s32[32,2]{0,1:T(2,128)S(1)}, s32[32,2]{0,1:T(2,128)}, u32[]{:S(2)}) copy-start(s32[32,2]{0,1:T(2,128)} %param.34) | copy-start | bytes 772
  244.9 37.8 %copy-start.14 = (bf16[32,4096]{1,0:T(8,128)(2,1)S(1)}, bf16[32,4096]{1,0:T(8,128)(2,1)}, u32[]{:S(2)}) copy-start(bf16[32,4096]{1,0:T(8,128)(2,1)} %param.32) | copy-start | bytes 786436
  244.9 39.0 %copy-start.22 = (f32[4096]{0:T(1024)S(1)}, f32[4096]{0:T(1024)}, u32[]{:S(2)}) copy-start(f32[4096]{0:T(1024)} %param.33) | copy-start | bytes 49156
  244.9 184.4 %reduce-scatter.5.cloned.1.call-start = ((), (), s32[]{:S(2)}) async-start(), calls=%async_computation.8 | async-start | bytes 3932160 | tf_op jit(solution)/shard_map/reduce_scatter | solution.py:187
  283.9 0.7 copy-start.9
  316.1 2.5 collective-permute-start.1
  321.5 36.4 %collective-permute-start.2 = (bf16[2,1,96,4096]{3,2,0,1:T(8,128)(2,1)S(1)}, bf16[2,1,96,4096]{3,2,0,1:T(8,128)(2,1)S(1)}, u32[]{:S(2)}, u32[]{:S(2)}) collective-permute-start(bf16[2,1,96,4096]{3,2,0,1:T(8,128)(2,1)S(1)} %get-tuple-element.195), channel_id=1, source_target_pairs={{0,2},{1,3},{2,0},{3,1},{4,6},{5,7},{6,4},{7,5},{8,10},{9,11},{10,... | collective-permute-start | bytes 4718600 | tf_op jit(solution)/shard_map/ppermute | solution.py:22
  357.9 1.2 copy-start.11
  393.1 44.2 %copy-start.26 = (f32[32,2]{0,1:T(2,128)S(1)}, f32[32,2]{0,1:T(2,128)}, u32[]{:S(2)}) copy-start(f32[32,2]{0,1:T(2,128)} %param.35) | copy-start | bytes 772
  431.5 31.3 %all-to-all-start.1 = ((bf16[8,12,4096]{2,1,0:T(8,128)(2,1)}), bf16[8,12,4096]{2,1,0:T(8,128)(2,1)S(1)}, u32[]{:S(2)}, u32[]{:S(2)}) async-start(bf16[8,12,4096]{2,1,0:T(8,128)(2,1)} %convert_element_type.72), calls=%async_computation.3 | async-start | bytes 2097152 | tf_op jit(solution)/shard_map/all_to_all | solution.py:193
  464.1 9.1 %copy-start.1 = (bf16[2048,544]{0,1:T(8,128)(2,1)S(1)}, bf16[2048,544]{0,1:T(8,128)(2,1)}, u32[]{:S(2)}) copy-start(bf16[2048,544]{0,1:T(8,128)(2,1)} %param.26) | copy-start | bytes 6684676
Sparse Core Ops, SparseCore 0:
  19.4 33.7 all-reduce.15
  111.6 40.5 all-gather.4
  154.9 38.8 all-gather.2
  245.0 37.5 reduce-scatter.2
  393.2 36.0 reduce-scatter.4
